TPU v7x, 128 devices: a whole 4x4x4 slice. The times are simulated.
128 devices in a mesh: path: 16 (over y_hi, z, core), trade: 8 (over y_lo, x).
Axes of the slice: x: 4, y: 4 (y_hi: 2, y_lo: 2; y = y_hi * 2 + y_lo), z: 4, core: 2. Of those that a mesh axis runs over, the one named last changes fastest.
Arguments:
- state: bfloat16 [3, 16384, 128], P(None, 'path'), may hold values from -5 to 5
- basis_projection_weight: bfloat16 [128, 256], replicated, may hold values from -0.5 to 0.5
- factor_node_loading: bfloat16 [128, 1024], replicated, may hold values from -0.011962891 to 0.011962891
- curve: float32 [1024], replicated, may hold values from 0.01 to 0.05
- discount: float32 [3, 16384], P(None, 'path'), may hold values from 0.7 to 1
- region: int32 [3, 16384, 32], P(None, 'path', 'trade'), may hold values from 0 to 2
- carry_in: float32 [16384, 32], P('path', 'trade'), may hold values from -1.5 to 2.5
- group_of: int32 [20000], P('trade'), may hold values from 0 to 31, as said below
- swap_start: int32 [20000], P('trade'), may hold values from 0 to 511
- swap_length: int32 [20000], P('trade'), may hold values from 8 to 511
- strike: float32 [20000], P('trade'), may hold values from 0.01 to 0.05
- notional: float32 [20000], P('trade'), may hold values from -0.6 to 0.6
- bucket_map: float32 [1024, 64], replicated, may hold values from -0.1875 to 0.1875
Outputs:
- values: float32 [16384, 32], P('path', 'trade')
- coefficients: float32 [3, 32, 256], P(None, 'trade')
- node_adjoint: float32 [1024], replicated
- bucketed: float32 [64], replicated
Inputs may be any that keep to these rules, and one draw needn't show every extreme that they name: `group_of`: trade t belongs to a group from (t // 2500) * 4 to (t // 2500) * 4 + 3.
All inputs are finite; a program needn't handle non-finite values.
Results may differ from a plain program's by a relative error of at most 0.005.
Values may be sent and summed in bfloat16 or wider, within the bound.
A program may use at most 128 MiB of HBM per device.

v0:
```python
import functools

import jax
import jax.numpy as jnp
from jax import lax
from jax.sharding import Mesh
from jax.sharding import PartitionSpec as P

EXD = 3
BASIS = 256
NODES = 1024
GRP_DEV = 4
PATH = ("path_0", "path_1", "path_2")
TRADE = ("trade_0", "trade_1")
PATH_TRADE = ("path_0", "path_1", "path_2", "trade_0", "trade_1")


ridge_share = 0.05
horizon = 30.0


def copy_for_each(x, axis):
    copies = jnp.broadcast_to(x, (lax.axis_size(axis), *x.shape))
    return lax.all_to_all(copies, axis, split_axis=0, concat_axis=0, tiled=True)


def over_copies(x, axis):
    return copy_for_each(x, axis).sum(axis=0)


def over_axes(x, axes):
    return functools.reduce(lax.psum, axes, x)


def node_grid():
    return horizon * (jnp.arange(NODES, dtype=jnp.float32) + 1.0) / NODES


def discount_curve(state_now, factor_node_loading, curve):
    shock = jnp.dot(state_now, factor_node_loading, preferred_element_type=jnp.float32)
    return jnp.exp(-node_grid()[None, :] * (curve[None, :] + shock))


def cash_matrix(swap_start, swap_length, strike, notional):
    nodes = jnp.arange(NODES, dtype=jnp.int32)[None, :]
    first = swap_start[:, None]
    final = first + swap_length[:, None]
    opening = (nodes == first).astype(jnp.float32)
    closing = (nodes == final).astype(jnp.float32)
    coupons = ((nodes > first) & (nodes <= final)).astype(jnp.float32)
    return notional[:, None] * (opening - closing - strike[:, None] * (horizon / NODES) * coupons)


def solve_groups(lower_factor, right_side_rows):
    column = right_side_rows[:, :, None]
    middle = lax.linalg.triangular_solve(lower_factor, column, left_side=True, lower=True)
    result = lax.linalg.triangular_solve(
        lower_factor, middle, left_side=True, lower=True, transpose_a=True
    )
    return result[:, :, 0]


def evaluate_basis(path_state_rows, basis_projection_weight):
    return jnp.tanh(
        jnp.einsum(
            "bjp,pl->bjl",
            path_state_rows,
            basis_projection_weight,
            preferred_element_type=jnp.float32,
        )
    ).astype(jnp.bfloat16)


def shards(
    state,
    basis_projection_weight,
    factor_node_loading,
    curve,
    discount,
    region,
    carry_in,
    group_of,
    swap_start,
    swap_length,
    strike,
    notional,
    bucket_map,
):
    path_total = state.shape[1] * lax.axis_size(PATH)
    offset = lax.axis_index(TRADE) * GRP_DEV
    members = (group_of[:, None] - offset == jnp.arange(GRP_DEV, dtype=jnp.int32)[None, :]).astype(
        jnp.float32
    )
    group_cash = jnp.dot(
        members.T,
        cash_matrix(swap_start, swap_length, strike, notional),
        precision=lax.Precision.HIGHEST,
    )
    ridge_term = ridge_share * path_total * jnp.eye(BASIS, dtype=jnp.float32)
    node_df = jnp.stack(
        [
            discount_curve(state[moment_matrix], factor_node_loading, curve)
            for moment_matrix in range(EXD)
        ]
    )
    features = evaluate_basis(state, basis_projection_weight)
    in_money_all = (region >= 1).astype(jnp.float32)
    holding_all = (region == 1).astype(jnp.float32)
    exercised_all = (region == 2).astype(jnp.float32)
    outside_all = (region == 0).astype(jnp.float32)

    def local_grams(moment_matrix):
        masked = features[moment_matrix][None] * in_money_all[moment_matrix].T[:, :, None].astype(
            jnp.bfloat16
        )
        return jnp.einsum(
            "gpk,pl->gkl", masked, features[moment_matrix], preferred_element_type=jnp.float32
        )

    def local_projection(moment_matrix, target):
        return jnp.dot(
            features[moment_matrix].T,
            (in_money_all[moment_matrix] * target).astype(jnp.bfloat16),
            preferred_element_type=jnp.float32,
        ).T

    final_target_value = discount[EXD - 1][:, None] * carry_in
    stacked = jnp.stack([local_grams(moment_matrix) for moment_matrix in range(EXD)])
    window_payload, last_summed = lax.psum(
        (stacked, local_projection(EXD - 1, final_target_value)), PATH
    )
    values = carry_in
    factor_list = [None] * EXD
    coefficient_list = [None] * EXD
    for moment_matrix in reversed(range(EXD)):
        payoff = jnp.dot(node_df[moment_matrix], group_cash.T, precision=lax.Precision.HIGHEST)
        target = discount[moment_matrix][:, None] * values
        grams = window_payload[moment_matrix]
        if moment_matrix == EXD - 1:
            projection = last_summed
        else:
            projection = over_copies(local_projection(moment_matrix, target), PATH)
        lower_factor = jnp.linalg.cholesky(grams + ridge_term[None])
        coefficient = solve_groups(lower_factor, projection)
        fitted = jnp.dot(
            features[moment_matrix],
            coefficient.T.astype(jnp.bfloat16),
            preferred_element_type=jnp.float32,
        )
        values = (
            exercised_all[moment_matrix] * payoff
            + holding_all[moment_matrix] * fitted
            + outside_all[moment_matrix] * target
        )
        factor_list[moment_matrix] = lower_factor
        coefficient_list[moment_matrix] = coefficient
    adjoint_value = jnp.full(values.shape, 1.0 / path_total, dtype=jnp.float32)
    node_total = jnp.zeros((NODES,), jnp.float32)
    for moment_matrix in range(EXD):
        weight = exercised_all[moment_matrix] * adjoint_value
        node_total = node_total + jnp.sum(
            group_cash * jnp.dot(weight.T, node_df[moment_matrix], precision=lax.Precision.HIGHEST),
            axis=0,
        )
        if moment_matrix < EXD - 1:
            local_pull = jnp.dot(
                features[moment_matrix].T,
                (holding_all[moment_matrix] * adjoint_value).astype(jnp.bfloat16),
                preferred_element_type=jnp.float32,
            ).T
            pulled = over_copies(local_pull, PATH)
            back = solve_groups(factor_list[moment_matrix], pulled)
            spread = jnp.dot(
                features[moment_matrix],
                back.T.astype(jnp.bfloat16),
                preferred_element_type=jnp.float32,
            )
            adjoint_value = discount[moment_matrix][:, None] * (
                outside_all[moment_matrix] * adjoint_value + in_money_all[moment_matrix] * spread
            )
    node_total = over_axes(node_total, PATH_TRADE)
    node_adjoint = -node_grid() * node_total
    bucketed = jnp.dot(node_adjoint[None, :], bucket_map, precision=lax.Precision.HIGHEST)[0]
    return (values, jnp.stack(coefficient_list), node_adjoint, bucketed)


def solution(mesh):
    torus = Mesh(
        mesh.devices.reshape(2, 4, 2, 2, 4), ("path_0", "path_1", "path_2", "trade_0", "trade_1")
    )
    in_specs = (
        P(None, PATH, None),
        P(),
        P(),
        P(),
        P(None, PATH),
        P(None, PATH, TRADE),
        P(PATH, TRADE),
        P(TRADE),
        P(TRADE),
        P(TRADE),
        P(TRADE),
        P(TRADE),
        P(),
    )
    out_specs = (P(PATH, TRADE), P(None, TRADE, None), P(), P())
    return jax.shard_map(
        shards, mesh=torus, in_specs=in_specs, out_specs=out_specs, check_vma=False
    )
```

profile of v0, /device:TPU:1, one launch (start us, length us, event | category | flops | bytes accessed | tf_op | source)
XLA Modules:
  0.0 1019.6 jit_solution(8482014038626432018)
XLA Ops:
  7.2 1.5 compare_convert_fusion.1
  8.7 1.7 tanh_convert_fusion
  11.2 9.4 all-to-all-start.2
  22.3 1.8 fusion.38
  25.7 2.1 pad_maximum_fusion
  30.0 33.1 %psum.50 = f32[4,256,1]{1,0,2:T(4,128)S(1)} all-reduce(f32[4,256,1]{1,0,2:T(4,128)S(1)} %convolution_bitcast_fusion), channel_id=1, replica_groups=mesh['path_0'=2,'path_1'=4,'path_2'=2,'trade_0'=2,'trade_1'=4] {'path_0'..., use_global_device_ids=true, to_apply=%region_5.0 | all-reduce | flops 1024 | bytes 8192 | tf_op jit(solution)/shard_map/psum | solution.py:129
  63.9 8.0 fusion
  71.9 3.2 fusion.66
  75.1 5.1 fusion.64
  81.0 4.8 fusion.60
  86.5 4.8 fusion.62
  92.6 83.7 %all-reduce.3.cloned.1.call-done = f32[3,4,256,256]{2,3,1,0:T(8,128)} async-done(((f32[3,4,256,256]{2,3,1,0:T(8,128)}), f32[3,4,256,256]{2,3,1,0:T(8,128)}) %all-reduce.3.cloned.1.call-update) | async-done | bytes 3145744 | tf_op jit(solution)/shard_map/psum | solution.py:129
  176.3 3.5 fusion.70
  179.8 2.6 copy.78
  182.5 2.5 copy.83
  185.0 3.6 fusion.72
  189.6 46.9 %custom-call.36 = f32[4,128,128]{2,1,0:T(8,128)S(1)} custom-call(f32[4,128,128]{2,1,0:T(8,128)S(1)} %cholesky.280), custom_call_target="Cholesky" | custom-call | tf_op jit(solution)/shard_map/jit(cholesky)/cholesky | solution.py:143
  236.5 1.7 cholesky.277
  238.2 47.7 %custom-call.33 = f32[4,128,128]{2,1,0:T(8,128)S(1)} custom-call(f32[4,128,128]{2,1,0:T(8,128)} %cholesky.277), custom_call_target="Cholesky" | custom-call | tf_op jit(solution)/shard_map/jit(cholesky)/cholesky | solution.py:143
  289.8 47.5 %custom-call.30 = f32[4,128,128]{2,1,0:T(8,128)} custom-call(f32[4,128,128]{2,1,0:T(8,128)S(1)} %cholesky.274), custom_call_target="Cholesky" | custom-call | tf_op jit(solution)/shard_map/jit(cholesky)/cholesky | solution.py:143
  338.5 1.9 select_bitcast_fusion.1
  340.4 40.9 %custom-call.34 = f32[4,1,128,128]{2,3,1,0:T(8,128)} custom-call(f32[4,1,128,128]{3,2,1,0:T(8,128)} %get-tuple-element.139), custom_call_target="InvertDiagBlocksLowerTriangular" | custom-call | tf_op jit(solution)/shard_map/jit(cholesky)/cholesky | solution.py:143
  381.3 2.2 constant_dynamic-update-slice_fusion.3
  383.5 2.3 convolution_subtract_fusion.1
  385.8 48.3 %custom-call.35 = f32[4,128,128]{2,1,0:T(8,128)} custom-call(f32[4,128,128]{2,1,0:T(8,128)} %convolution_subtract_fusion.1), custom_call_target="Cholesky" | custom-call | tf_op jit(solution)/shard_map/jit(cholesky)/cholesky | solution.py:143
  434.1 40.7 %custom-call.37 = f32[4,1,128,128]{2,3,1,0:T(8,128)} custom-call(f32[4,1,128,128]{3,2,1,0:T(8,128)} %get-tuple-element.140), custom_call_target="InvertDiagBlocksLowerTriangular" | custom-call | tf_op jit(solution)/shard_map/jit(cholesky)/cholesky | solution.py:143
  476.3 2.3 convolution_subtract_fusion
  478.6 48.7 %custom-call.38 = f32[4,128,128]{2,1,0:T(8,128)} custom-call(f32[4,128,128]{2,1,0:T(8,128)} %convolution_subtract_fusion), custom_call_target="Cholesky" | custom-call | tf_op jit(solution)/shard_map/jit(cholesky)/cholesky | solution.py:143
  527.4 40.7 %custom-call.31 = f32[4,1,128,128]{2,3,1,0:T(8,128)} custom-call(f32[4,1,128,128]{3,2,1,0:T(8,128)} %get-tuple-element.141), custom_call_target="InvertDiagBlocksLowerTriangular" | custom-call | tf_op jit(solution)/shard_map/jit(cholesky)/cholesky | solution.py:143
  568.1 2.1 cholesky.201
  570.2 2.1 constant_dynamic-update-slice_fusion.5
  572.4 2.3 convolution_subtract_fusion.2
  574.7 48.3 %custom-call.32 = f32[4,128,128]{2,1,0:T(8,128)} custom-call(f32[4,128,128]{2,1,0:T(8,128)} %convolution_subtract_fusion.2), custom_call_target="Cholesky" | custom-call | tf_op jit(solution)/shard_map/jit(cholesky)/cholesky | solution.py:143
  623.0 2.2 select_reduce_fusion.4
  626.2 3.8 select_select_fusion.2
  630.1 4.2 while.22
  635.1 79.6 %custom-call.44 = f32[4,2,128,128]{2,3,1,0:T(8,128)S(1)} custom-call(f32[4,2,128,128]{3,2,1,0:T(8,128)} %bitcast.552), custom_call_target="InvertDiagBlocksLowerTriangular" | custom-call | tf_op jit(solution)/shard_map/triangular_solve/custom-call.4 | solution.py:57
  719.2 5.4 fusion.67
  725.5 8.6 while.20
  726.7 3.1 bitcast_dynamic-update-slice_fusion.6
  731.0 3.0 bitcast_dynamic-update-slice_fusion.6
  734.1 80.0 %custom-call.40 = f32[4,2,128,128]{2,3,1,0:T(8,128)} custom-call(f32[4,2,128,128]{3,2,1,0:T(8,128)} %bitcast.553), custom_call_target="InvertDiagBlocksLowerTriangular" | custom-call | tf_op jit(solution)/shard_map/triangular_solve/custom-call.4 | solution.py:57
  815.0 8.5 while.21
  816.2 3.1 bitcast_dynamic-update-slice_fusion.7
  820.5 3.0 bitcast_dynamic-update-slice_fusion.7
  823.5 80.2 %custom-call.42 = f32[4,2,128,128]{2,3,1,0:T(8,128)} custom-call(f32[4,2,128,128]{3,2,1,0:T(8,128)} %bitcast.554), custom_call_target="InvertDiagBlocksLowerTriangular" | custom-call | tf_op jit(solution)/shard_map/triangular_solve/custom-call.4 | solution.py:57
  905.0 1.5 fusion.109
  908.5 1.5 fusion.108
  911.3 2.1 fusion.107
  913.9 7.5 all-to-all-start.3
  924.5 4.4 all-to-all-done.3
  929.5 4.3 all-to-all-start
  935.9 1.5 fusion.133
  944.0 4.8 fusion.68
  951.0 1.5 fusion.137
  959.2 5.3 psum.51
  964.5 8.6 psum.52
  973.1 5.7 psum.53
  978.7 3.8 psum.54
  982.5 8.4 psum.55
  991.5 8.1 all-to-all-start.1
  999.6 1.8 convolution_bitcast_fusion.6
  1002.1 4.9 all-to-all-done.1
  1009.6 1.6 fusion.53
  (182 shorter events, 65.8 us)
Async XLA Ops:
  7.2 56.0 %copy-start = (bf16[128,1024]{1,0:T(8,128)(2,1)S(1)}, bf16[128,1024]{1,0:T(8,128)(2,1)}, u32[]{:S(2)}) copy-start(bf16[128,1024]{1,0:T(8,128)(2,1)} %param.20) | copy-start | bytes 786436
  8.7 12.0 %copy-start.9 = (f32[3,1024,4]{1,2,0:T(4,128)}, f32[3,1024,4]{1,2,0:T(4,128)S(1)}, u32[]{:S(2)}) copy-start(f32[3,1024,4]{1,2,0:T(4,128)S(1)} %get-tuple-element.133) | copy-start | bytes 147460
  11.2 80.5 %all-to-all-start.2 = ((f32[16,4,256]{2,1,0:T(4,128)}), f32[16,4,256]{2,1,0:T(4,128)}, u32[]{:S(2)}, u32[]{:S(2)}) async-start(f32[16,4,256]{2,1,0:T(4,128)} %broadcast_in_dim.33), calls=%async_computation.2 | async-start | bytes 131072 | tf_op jit(solution)/shard_map/all_to_all | solution.py:24
  20.7 155.7 %all-reduce.3.cloned.1.call-start = ((), (), s32[]{:S(2)}) async-start(), calls=%async_computation.4 | async-start | bytes 6291456 | tf_op jit(solution)/shard_map/psum | solution.py:129
  25.6 3.6 copy-start.21
  25.6 3.6 copy-start.25
  25.6 4.2 copy-start.16
  25.6 37.5 %copy-start.22 = (s32[2500]{0:T(1024)S(1)}, s32[2500]{0:T(1024)}, u32[]{:S(2)}) copy-start(s32[2500]{0:T(1024)} %param.25) | copy-start | bytes 30004
  25.7 37.5 %copy-start.23 = (s32[2500]{0:T(1024)S(1)}, s32[2500]{0:T(1024)}, u32[]{:S(2)}) copy-start(s32[2500]{0:T(1024)} %param.27) | copy-start | bytes 30004
  25.7 37.5 %copy-start.24 = (s32[2500]{0:T(1024)S(1)}, s32[2500]{0:T(1024)}, u32[]{:S(2)}) copy-start(s32[2500]{0:T(1024)} %param.26) | copy-start | bytes 30004
  25.7 37.5 %copy-start.6 = (bf16[3,1024,128]{2,1,0:T(8,128)(2,1)S(1)}, bf16[3,1024,128]{2,1,0:T(8,128)(2,1)}, u32[]{:S(2)}) copy-start(bf16[3,1024,128]{2,1,0:T(8,128)(2,1)} %param.18) | copy-start | bytes 2359300
  27.8 36.1 %copy-start.27 = (f32[2500]{0:T(1024)S(1)}, f32[2500]{0:T(1024)}, u32[]{:S(2)}) copy-start(f32[2500]{0:T(1024)} %param.29) | copy-start | bytes 30004
  29.8 42.1 %copy-start.14 = (f32[1,1024]{1,0:T(1,128)}, f32[1,1024]{1,0:T(1,128)S(1)}, u32[]{:S(2)}) copy-start(f32[1,1024]{1,0:T(1,128)S(1)} %get-tuple-element.137) | copy-start | bytes 12292
  63.1 8.8 copy-start.20
  63.9 8.0 copy-start.8
  81.0 5.5 copy-start.1
  86.4 4.8 copy-start.2
  188.6 1.0 copy-start.5
  288.7 1.1 copy-start.4
  623.0 7.0 copy-start.29
  625.2 1.0 copy-start.3
  634.3 0.8 copy-start.7
  634.3 80.4 %copy-start.28 = (s32[2,2]{1,0:T(2,128)}, s32[2,2]{1,0:T(2,128)S(1)}, u32[]{:S(2)}) copy-start(s32[2,2]{1,0:T(2,128)S(1)} %get-tuple-element.294) | copy-start | bytes 52
  724.6 179.1 %slice-start = ((f32[4,256,1]{1,0,2:T(4,128)}), f32[4,128,1]{1,0,2:T(4,128)S(1)}, s32[]{:S(2)}) async-start(f32[4,256,1]{1,0,2:T(4,128)} %copy-done.20), calls=%async_computation.5 | async-start | bytes 4096 | tf_op jit(solution)/shard_map/triangular_solve/slice.6 | solution.py:56
  913.9 14.9 %all-to-all-start.3 = ((f32[16,4,256]{2,1,0:T(4,128)}), f32[16,4,256]{2,1,0:T(4,128)}, u32[]{:S(2)}, u32[]{:S(2)}) async-start(f32[16,4,256]{2,1,0:T(4,128)} %broadcast_in_dim.65), calls=%async_computation.3 | async-start | bytes 131072 | tf_op jit(solution)/shard_map/all_to_all | solution.py:24
  922.4 0.6 copy-start.17
  929.5 19.3 %all-to-all-start = ((f32[16,4,256]{2,1,0:T(4,128)}), f32[16,4,256]{2,1,0:T(4,128)}, u32[]{:S(2)}, u32[]{:S(2)}) async-start(f32[16,4,256]{2,1,0:T(4,128)} %broadcast_in_dim.27), calls=%async_computation | async-start | bytes 131072 | tf_op jit(solution)/shard_map/all_to_all | solution.py:24
  940.2 19.0 %copy-start.13 = (f32[1024]{0:T(1024)S(1)}, f32[1024]{0:T(1024)}, u32[]{:S(2)}) copy-start(f32[1024]{0:T(1024)} %fusion.66) | copy-start | bytes 12292
  940.2 19.0 %copy-start.15 = (f32[1024]{0:T(1024)S(1)}, f32[1024]{0:T(1024)}, u32[]{:S(2)}) copy-start(f32[1024]{0:T(1024)} %fusion.67) | copy-start | bytes 12292
  943.9 14.1 %copy-start.11 = (f32[1024,4]{0,1:T(4,128)S(1)}, f32[1024,4]{0,1:T(4,128)}, u32[]{:S(2)}) copy-start(f32[1024,4]{0,1:T(4,128)} %fusion.62) | copy-start | bytes 49156
  944.0 14.1 %copy-start.18 = (f32[1024,4]{0,1:T(4,128)S(1)}, f32[1024,4]{0,1:T(4,128)}, u32[]{:S(2)}) copy-start(f32[1024,4]{0,1:T(4,128)} %copy-done.17) | copy-start | bytes 49156
  944.0 65.7 %copy-start.10 = (f32[1024,4]{0,1:T(4,128)S(1)}, f32[1024,4]{0,1:T(4,128)}, u32[]{:S(2)}) copy-start(f32[1024,4]{0,1:T(4,128)} %fusion.64) | copy-start | bytes 49156
  958.0 33.5 %copy-start.26 = (f32[4,1,128]{2,1,0:T(1,128)}, f32[4,1,128]{2,1,0:T(1,128)S(1)}, u32[]{:S(2)}) copy-start(f32[4,1,128]{2,1,0:T(1,128)S(1)} %fusion.120) | copy-start | bytes 6148
  959.0 32.5 %copy-start.19 = (f32[1024,4]{0,1:T(4,128)}, f32[1024,4]{0,1:T(4,128)S(1)}, u32[]{:S(2)}) copy-start(f32[1024,4]{0,1:T(4,128)S(1)} %fusion.56) | copy-start | bytes 49156
  990.9 21.7 %copy-start.12 = (f32[1024]{0:T(1024)}, f32[1024]{0:T(1024)S(1)}, u32[]{:S(2)}) copy-start(f32[1024]{0:T(1024)S(1)} %fusion.187) | copy-start | bytes 12292
  991.5 15.5 %all-to-all-start.1 = ((f32[16,4,256]{2,1,0:T(4,128)}), f32[16,4,256]{2,1,0:T(4,128)S(1)}, u32[]{:S(2)}, u32[]{:S(2)}) async-start(f32[16,4,256]{2,1,0:T(4,128)} %broadcast_in_dim.29), calls=%async_computation.1 | async-start | bytes 131072 | tf_op jit(solution)/shard_map/all_to_all | solution.py:24
Sparse Core Ops, SparseCore 0:
  28.0 148.3 all-reduce.2
where the time goes:
time: 1030 us; the launch traced here: 1020 us
  other arithmetic  679 us (66%)
  matrix products  95.5 us (9%)
  waiting for transfers between devices  93 us (9%)
  blocking collectives  64.8 us (6%)
  local copies, waits for them, and re-layouts  43.1 us (4%)
  starting transfers between devices  29.4 us (3%)
  between operations  14.9 us (1%)
    another operation x22, other arithmetic, shards(): lower_factor = jnp.linalg.cholesky(grams + ridge_term[None])  415 us
    another operation x11, other arithmetic, solve_groups(): lax.linalg.triangular_solve(lower_factor, middle, left_side=True, lower=T...  245 us
    psum x1, waiting for transfers between devices, shards(): lax.psum((stacked, local_projection(EXD - 1, final_target_value)), PATH)  83.7 us
    psum x1, blocking collectives, shards(): lax.psum((stacked, local_projection(EXD - 1, final_target_value)), PATH)  33.1 us
    psum x5, blocking collectives, over_axes(): return functools.reduce(lax.psum, axes, x)  31.7 us
    all_to_all x4, starting transfers between devices, copy_for_each(): return lax.all_to_all(copies, axis, split_axis=0, concat_axis=0, tiled=True)  29.3 us
    another operation x22, local copies, waits for them, and re-layouts, solve_groups(): lax.linalg.triangular_solve(lower_factor, middle, left_side=True, lower=T...  23.1 us
  transfers between devices with their start and end apart: 5, of which 3 were waited for; matrix products, arithmetic and copies ran while one was open for 6% of the time, Pallas kernels for 0%

commit v1 on v0

v1 whole, which is shorter than its diff:
```python
import jax
import jax.numpy as jnp
from jax import lax
from jax.experimental import pallas as pl
from jax.experimental.pallas import tpu as pltpu
from jax.sharding import Mesh
from jax.sharding import PartitionSpec as P

EXD = 3
BASIS = 256
NODES = 1024
FAC = 128
GRP = 4
LOCAL = 1024
TRADES = 2500
TPAD = 2560
PATHS = 16384
PATH = ("path_0", "path_1", "path_2")
TRADE = ("trade_0", "trade_1")
MESH = pl.DeviceIdType.MESH
HIGH = lax.Precision.HIGHEST
F32 = jnp.float32
BF16 = jnp.bfloat16
ROWS = 264

ridge_share = 0.05
horizon = 30.0
BOUND = (BASIS + ridge_share) * PATHS

NT = (((1,), (1,)), ((), ()))
NN = (((1,), (0,)), ((), ()))


def dot(a, b, dims=NN, precision=None):
    return lax.dot_general(a, b, dims, precision=precision, preferred_element_type=F32)


def split3(x):
    one = x.astype(BF16).astype(F32)
    rest = x - one
    two = rest.astype(BF16).astype(F32)
    return one, two, (rest - two).astype(BF16).astype(F32)


def stack3(x):
    pieces = split3(x)
    return jnp.concatenate([*pieces, jnp.zeros_like(x)], axis=0).astype(BF16)


def polynomials():
    low, high = ridge_share * PATHS / BOUND, 1.0
    steps = []
    while not steps or high - 1.0 > 2e-6:
        width, middle = high - low, high + low
        scale = 2.0 * (middle / width) ** 2 - 1.0
        steps.append((8.0 * middle / width**2 / scale, 8.0 / width**2 / scale))
        low, high = 1.0 - 1.0 / scale, 1.0 + 1.0 / scale
    return steps


def dot3(a, b):
    a_hi, b_hi = a.astype(BF16), b.astype(BF16)
    a_lo = (a - a_hi.astype(F32)).astype(BF16)
    b_lo = (b - b_hi.astype(F32)).astype(BF16)
    return dot(a_hi, b_hi) + (dot(a_hi, b_lo) + dot(a_lo, b_hi))


def invert(a):
    eye = (
        lax.broadcasted_iota(jnp.int32, (BASIS, BASIS), 0) == lax.broadcasted_iota(jnp.int32, (BASIS, BASIS), 1)
    ).astype(F32)
    a = a * (1.0 / BOUND)
    (alpha, beta), *others, last = polynomials()
    inverse = alpha * eye - beta * a
    product = dot3(a, inverse)
    for alpha, beta in others:
        both = dot3(jnp.concatenate([inverse, product], axis=0), alpha * eye - beta * product)
        inverse, product = both[:BASIS], both[BASIS:]
    alpha, beta = last
    product = dot(a, inverse, NN, HIGH)
    return dot(inverse, alpha * eye - beta * product, NN, HIGH) * (1.0 / BOUND)


def kernel(
    state,
    weight,
    loading,
    curve,
    discount,
    region,
    carry,
    group_of,
    swap_start,
    swap_length,
    strike,
    notional,
    bucket_map,
    values_out,
    coefficient_out,
    node_out,
    bucket_out,
    ft,
    rhs,
    away,
    home,
    got_core,
    got_z,
    got_y,
    df_hi,
    df_lo,
    ints,
    floats,
    payoff,
    inverse_ref,
    answer_src,
    answer_a,
    answer_b,
    answer_c,
    part_b,
    part_c,
    gather_b,
    gather_c,
    node_one,
    node_two,
    core_send,
    core_recv,
    z_send,
    z_recv,
    y_send,
    y_recv,
    a_send,
    a_recv,
    b_send,
    b_recv,
    bb_send,
    bb_recv,
    c_send,
    c_recv,
    cc_send,
    cc_recv,
    n1_send,
    n1_recv,
    n2_send,
    n2_recv,
):
    yh = lax.axis_index("path_0")
    z = lax.axis_index("path_1")
    core = lax.axis_index("path_2")
    yl = lax.axis_index("trade_0")
    x = lax.axis_index("trade_1")
    me = yh * 8 + z * 2 + core
    tme = yl * 4 + x
    mine = core * 2 + yh

    def path_id(p):
        return {"path_0": p // 8, "path_1": (p // 2) % 4, "path_2": p % 2}

    def trade_id(t):
        return {"trade_0": t // 4, "trade_1": t % 4}

    def remote(src, dst, send, recv, device):
        return pltpu.make_async_remote_copy(
            src_ref=src, dst_ref=dst, send_sem=send, recv_sem=recv, device_id=device, device_id_type=MESH
        )

    barrier = pltpu.get_barrier_semaphore()
    for k in range(1, 16):
        pl.semaphore_signal(barrier, inc=1, device_id=path_id((me + k) % 16), device_id_type=MESH)
    for k in range(1, 8):
        pl.semaphore_signal(barrier, inc=1, device_id=trade_id((tme + k) % 8), device_id_type=MESH)

    def features(i, _):
        chunk = state[pl.ds(pl.multiple_of(i * 256, 256), 256), :]
        wide = lax.dot_general(weight[...], chunk, (((0,), (1,)), ((), ())), preferred_element_type=F32)
        ft[i // 4, :, pl.ds(pl.multiple_of((i % 4) * 256, 256), 256)] = jnp.tanh(wide).astype(BF16)
        return 0

    lax.fori_loop(0, 12, features, 0)

    def masks(d):
        r = region[d]
        return (
            (r >= 1).astype(F32),
            (r == 1).astype(F32),
            (r == 2).astype(F32),
            (r == 0).astype(F32),
        )

    def project(rows8, d):
        return dot(rows8.astype(BF16), ft[d], NT)

    zero4 = jnp.zeros((4, LOCAL), F32)
    target2 = discount[2:3, :] * carry[...]
    rhs[2] = project(jnp.concatenate([masks(2)[0] * target2, zero4], axis=0), 2)
    rhs[1] = jnp.zeros((8, BASIS), F32)
    rhs[0] = project(jnp.concatenate([masks(0)[1] * (1.0 / PATHS), zero4], axis=0), 0)

    r128 = lax.broadcasted_iota(jnp.int32, (128, 128), 0)
    c128 = lax.broadcasted_iota(jnp.int32, (128, 128), 1)

    def gram(d, g, out, slot):
        mask = jnp.where(region[d, pl.ds(g, 1), :] >= 1, 1.0, 0.0).astype(BF16)
        f = ft[d]
        masked = f * mask
        top = dot(masked[0:128], f[0:128], NT)
        low = dot(masked[128:256], f, NT)
        last = low[:, 128:256]
        out[slot, 0:128, :] = jnp.where(r128 >= c128, top, last)
        out[slot, 128:256, :] = low[:, 0:128]
        diagonal = jnp.sum(jnp.where(r128 == c128, last, 0.0), axis=0, keepdims=True)
        right = rhs[d, pl.ds(g, 1), :]
        out[slot, 256:264, :] = jnp.concatenate(
            [diagonal, right[:, 0:128], right[:, 128:256], jnp.zeros((5, 128), F32)], axis=0
        )

    pl.semaphore_wait(barrier, 22)

    def core_copy(i):
        return remote(away.at[i], got_core.at[i], core_send.at[i], core_recv.at[i], {"path_2": 1 - core})

    def send_away(i, _):
        gram(i // 2, (1 - core) * 2 + i % 2, away, i)
        core_copy(i).start()
        return 0

    lax.fori_loop(0, 6, send_away, 0)

    def keep_home(i, _):
        gram(i // 2, core * 2 + i % 2, home, i)
        return 0

    lax.fori_loop(0, 6, keep_home, 0)

    def z_copy(i, d):
        slot = (z - d + 3) % 4
        at = slot * 2 + i % 2
        return remote(home.at[i], got_z.at[at], z_send.at[i], z_recv.at[at], {"path_1": d})

    def send_z(i, _):
        d = i // 2
        core_copy(i).wait()
        home[i] = home[i] + got_core[i]

        @pl.when(z != d)
        def _():
            z_copy(i, d).start()

        return 0

    lax.fori_loop(0, 6, send_z, 0)

    ints[...] = jnp.zeros_like(ints)
    floats[...] = jnp.zeros_like(floats)
    starts, amounts = swap_start[...].reshape(1, TRADES), notional[...].reshape(1, TRADES)
    ints[0:1, 0:TRADES] = group_of[...].reshape(1, TRADES) - tme * GRP
    ints[1:2, 0:TRADES] = starts
    ints[2:3, 0:TRADES] = starts + swap_length[...].reshape(1, TRADES)
    floats[0:1, 0:TRADES] = amounts
    floats[1:2, 0:TRADES] = amounts * (strike[...].reshape(1, TRADES) * (horizon / NODES))
    i32 = lax.broadcasted_iota(jnp.int32, (32, 512), 0)
    i128 = lax.broadcasted_iota(jnp.int32, (128, 512), 0)

    def histogram(i, total):
        span = pl.ds(pl.multiple_of(i * 512, 512), 512)
        group = ints[0:1, span]
        pieces = [*split3(floats[0:1, span]), *split3(floats[1:2, span])]
        for row, sign in ((1, 1.0), (2, -1.0)):
            key = ints[row : row + 1, span]
            hit = i32 == (key // 128) * 4 + group
            left = jnp.concatenate([jnp.where(hit, sign * piece, 0.0) for piece in pieces], axis=0).astype(BF16)
            right = (i128 == key % 128).astype(F32).astype(BF16)
            total = total + dot(left, right, NT)
        return total

    table = lax.fori_loop(0, 5, histogram, jnp.zeros((192, 128), F32))
    steps = table[0:32] + table[32:64] + table[64:96]
    slopes = table[96:128] + table[128:160] + table[160:192]
    before = (r128 < c128).astype(F32)
    ra = lax.broadcasted_iota(jnp.int32, (32, 32), 0)
    ca = lax.broadcasted_iota(jnp.int32, (32, 32), 1)
    earlier = ((ca // 4 < ra // 4) & (ca % 4 == ra % 4)).astype(F32)
    coupon = dot(slopes, before, NN, HIGH) + jnp.sum(dot(earlier, slopes, NN, HIGH), axis=1, keepdims=True)
    flat = steps - coupon
    cash = jnp.concatenate([flat[4 * a : 4 * a + 4, :] for a in range(8)], axis=1)
    cash_stack = stack3(cash)

    times = (lax.broadcasted_iota(jnp.int32, (1, NODES), 1).astype(F32) + 1.0) * (horizon / NODES)
    curve_row = curve[...]

    def sum3(t):
        return t[0:4] + t[4:8] + t[8:12]

    def discounting(i, _):
        span = pl.ds(pl.multiple_of(i * 256, 256), 256)
        shock = dot(state[span, :], loading[...])
        factor = jnp.exp(-times * (curve_row + shock))
        hi = factor.astype(BF16)
        lo = (factor - hi.astype(F32)).astype(BF16)
        df_hi[span, :] = hi
        df_lo[span, :] = lo
        payoff[i] = sum3(dot(cash_stack, hi, NT) + dot(cash_stack, lo, NT))
        return 0

    lax.fori_loop(0, 12, discounting, 0)

    def node_sum(w, d):
        stack = stack3(w)
        span = pl.ds(d * LOCAL, LOCAL)
        t = sum3(dot(stack, df_hi[span, :]) + dot(stack, df_lo[span, :]))
        return jnp.sum(cash * t, axis=0, keepdims=True)

    @pl.when(z < 3)
    def _():
        for j in range(2):
            total = home[z * 2 + j]
            for slot in range(3):
                z_copy_wait = remote(
                    home.at[0], got_z.at[slot * 2 + j], z_send.at[0], z_recv.at[slot * 2 + j], {"path_1": 0}
                )
                z_copy_wait.wait_recv()
                total = total + got_z[slot * 2 + j]
            home[z * 2 + j] = total

    def y_copy():
        return remote(home.at[z * 2 + 1 - yh], got_y, y_send, y_recv, {"path_0": 1 - yh})

    @pl.when(z < 3)
    def _():
        y_copy().start()

    in0, hold0, ex0, out0 = masks(0)
    bar0 = jnp.full((4, LOCAL), 1.0 / PATHS, F32)
    node_total = node_sum(ex0 * bar0, 0)

    def solve(rows8):
        return dot(rows8, inverse_ref[...], NN, HIGH)

    def broadcast(dst, sends, recvs, at):
        def go(k, _):
            remote(answer_src, dst.at[at], sends.at[k - 1], recvs.at[at], path_id((me + k) % 16)).start()
            return 0

        lax.fori_loop(1, 16, go, 0)

    def broadcast_done(dst, sends, recvs, at):
        def go(k, _):
            remote(answer_src, dst.at[at], sends.at[k - 1], recvs.at[at], path_id((me + k) % 16)).wait_send()
            return 0

        lax.fori_loop(1, 16, go, 0)

    def collect(dst, sends, recvs, at, owner):
        @pl.when(me != owner)
        def _():
            remote(answer_src, dst.at[at], sends.at[0], recvs.at[at], path_id(owner)).wait_recv()

    def owner_of(d, g):
        return (g % 2) * 8 + d * 2 + g // 2

    @pl.when(z < 3)
    def _():
        y_copy().wait()
        packed = home[z * 2 + yh] + got_y[...]
        mix = packed[0:128]
        flip = mix.T
        b = packed[128:256]
        ridge = jnp.where(r128 == c128, ridge_share * PATHS, 0.0)
        a = jnp.where(r128 >= c128, mix, flip) + ridge
        c = jnp.where(r128 < c128, mix, jnp.where(r128 > c128, flip, packed[256:257])) + ridge
        full = jnp.concatenate(
            [jnp.concatenate([a, b.T], axis=1), jnp.concatenate([b, c], axis=1)], axis=0
        )
        inverse_ref[...] = invert(full)

        @pl.when(z != 1)
        def _():
            at = (1 - z // 2) * 4 + mine
            row = jnp.concatenate([packed[257:258], packed[258:259]], axis=1)
            answer = solve(jnp.broadcast_to(row, (8, BASIS)))
            answer_src[...] = answer
            answer_a[at] = answer
            broadcast(answer_a, a_send, a_recv, at)

    for g in range(4):
        collect(answer_a, a_send, a_recv, g, owner_of(2, g))
        collect(answer_a, a_send, a_recv, 4 + g, owner_of(0, g))

    def pick(buffer, base, row):
        return jnp.concatenate(
            [buffer[base + g, row + (g if row >= 0 else 1) : row + (g if row >= 0 else 1) + 1, :] for g in range(4)],
            axis=0,
        )

    def payoff_of(d):
        return jnp.concatenate([payoff[4 * d + k] for k in range(4)], axis=1)

    def fit(coefficient, d):
        stacked = jnp.concatenate([coefficient, jnp.zeros_like(coefficient)], axis=0).astype(BF16)
        return dot(stacked, ft[d])[0:4]

    coef2 = pick(answer_a, 0, -1)
    back0 = pick(answer_a, 4, -1)
    coefficient_out[2] = coef2
    in1, hold1, ex1, out1 = masks(1)
    in2, hold2, ex2, out2 = masks(2)
    values2 = ex2 * payoff_of(2) + hold2 * fit(coef2, 2) + out2 * target2
    bar1 = discount[0:1, :] * (out0 * bar0 + in0 * fit(back0, 0))
    target1 = discount[1:2, :] * values2
    part_b[...] = project(jnp.concatenate([in1 * target1, hold1 * bar1], axis=0), 1)
    gather_b[me] = part_b[...]

    def gather(src, dst, sends, recvs, d):
        for g in range(4):
            owner = owner_of(d, g)

            @pl.when(me != owner)
            def _():
                remote(src, dst.at[me], sends.at[g], recvs.at[me], path_id(owner)).start()

    def gather_sent(src, dst, sends, recvs, d):
        for g in range(4):
            owner = owner_of(d, g)

            @pl.when(me != owner)
            def _():
                remote(src, dst.at[me], sends.at[g], recvs.at[me], path_id(owner)).wait_send()

    def gathered(src, dst, sends, recvs):
        def go(k, _):
            p = (me + k) % 16
            remote(src, dst.at[p], sends.at[0], recvs.at[p], path_id(p)).wait_recv()
            return 0

        lax.fori_loop(1, 16, go, 0)
        total = dst[0]
        for p in range(1, 16):
            total = total + dst[p]
        return total

    gather(part_b, gather_b, b_send, b_recv, 1)
    node_total = node_total + node_sum(ex1 * bar1, 1)

    @pl.when(z == 1)
    def _():
        answer = solve(gathered(part_b, gather_b, b_send, b_recv))
        answer_src[...] = answer
        answer_b[mine] = answer
        broadcast(answer_b, bb_send, bb_recv, mine)

    for g in range(4):
        collect(answer_b, bb_send, bb_recv, g, owner_of(1, g))
    coef1 = pick(answer_b, 0, 0)
    back1 = pick(answer_b, 0, 4)
    coefficient_out[1] = coef1
    values1 = ex1 * payoff_of(1) + hold1 * fit(coef1, 1) + out1 * target1
    target0 = discount[0:1, :] * values1
    part_c[...] = project(jnp.concatenate([in0 * target0, zero4], axis=0), 0)
    gather_c[me] = part_c[...]
    gather(part_c, gather_c, c_send, c_recv, 0)

    @pl.when(z == 0)
    def _():
        answer = solve(gathered(part_c, gather_c, c_send, c_recv))
        broadcast_done(answer_a, a_send, a_recv, 4 + mine)
        answer_src[...] = answer
        answer_c[mine] = answer
        broadcast(answer_c, cc_send, cc_recv, mine)

    bar2 = discount[1:2, :] * (out1 * bar1 + in1 * fit(back1, 1))
    node_total = node_total + node_sum(ex2 * bar2, 2)
    tile = jnp.concatenate([node_total[:, 128 * k : 128 * k + 128] for k in range(8)], axis=0)
    node_one[me] = tile

    def one_copy(k):
        return remote(
            node_one.at[me], node_one.at[me], n1_send.at[k - 1], n1_recv.at[me], path_id((me + k) % 16)
        )

    def one_arrival(k):
        p = (me + k) % 16
        return remote(node_one.at[me], node_one.at[p], n1_send.at[0], n1_recv.at[p], path_id(p))

    def two_copy(k):
        return remote(
            node_two.at[tme], node_two.at[tme], n2_send.at[k - 1], n2_recv.at[tme], trade_id((tme + k) % 8)
        )

    def two_arrival(k):
        t = (tme + k) % 8
        return remote(node_two.at[tme], node_two.at[t], n2_send.at[0], n2_recv.at[t], trade_id(t))

    def run(first, last, f):
        def go(k, _):
            f(k)
            return 0

        lax.fori_loop(first, last, go, 0)

    run(1, 16, lambda k: one_copy(k).start())
    run(1, 16, lambda k: one_arrival(k).wait_recv())
    total = node_one[0]
    for p in range(1, 16):
        total = total + node_one[p]
    node_two[tme] = total
    run(1, 8, lambda k: two_copy(k).start())

    for g in range(4):
        collect(answer_c, cc_send, cc_recv, g, owner_of(0, g))
    coef0 = pick(answer_c, 0, 0)
    coefficient_out[0] = coef0
    values_out[...] = ex0 * payoff_of(0) + hold0 * fit(coef0, 0) + out0 * target0

    run(1, 8, lambda k: two_arrival(k).wait_recv())
    total = node_two[0]
    for t in range(1, 8):
        total = total + node_two[t]
    grid = (
        lax.broadcasted_iota(jnp.int32, (8, 128), 0) * 128 + lax.broadcasted_iota(jnp.int32, (8, 128), 1)
    ).astype(F32)
    adjoint = -((grid + 1.0) * (horizon / NODES)) * total
    node_out[...] = adjoint
    line = jnp.concatenate([adjoint[k : k + 1, :] for k in range(8)], axis=1)
    bucket_out[...] = dot(jnp.broadcast_to(line, (8, NODES)), bucket_map[...], NT, HIGH)

    def z_sent(i, _):
        d = i // 2

        @pl.when(z != d)
        def _():
            z_copy(i, d).wait_send()

        return 0

    lax.fori_loop(0, 6, z_sent, 0)
    gather_sent(part_b, gather_b, b_send, b_recv, 1)
    gather_sent(part_c, gather_c, c_send, c_recv, 0)

    @pl.when(z == 2)
    def _():
        broadcast_done(answer_a, a_send, a_recv, mine)

    @pl.when(z == 1)
    def _():
        broadcast_done(answer_b, bb_send, bb_recv, mine)

    @pl.when(z == 0)
    def _():
        broadcast_done(answer_c, cc_send, cc_recv, mine)

    run(1, 16, lambda k: one_copy(k).wait_send())
    run(1, 8, lambda k: two_copy(k).wait_send())


def finish(values, coefficients, node, bucketed, values_out, coefficients_out, node_out, bucketed_out):
    values_out[...] = values[...]
    coefficients_out[...] = coefficients[...]
    node_out[...] = node[...].reshape(NODES)
    bucketed_out[...] = bucketed[0:1, :].reshape(64)


def shards(
    state,
    basis_projection_weight,
    factor_node_loading,
    curve,
    discount,
    region,
    carry_in,
    group_of,
    swap_start,
    swap_length,
    strike,
    notional,
    bucket_map,
):
    vmem = pl.BlockSpec(memory_space=pltpu.VMEM)
    dma = pltpu.SemaphoreType.DMA
    values, coefficients, node, bucketed = pl.pallas_call(
        kernel,
        out_shape=(
            jax.ShapeDtypeStruct((GRP, LOCAL), F32),
            jax.ShapeDtypeStruct((EXD, GRP, BASIS), F32),
            jax.ShapeDtypeStruct((8, 128), F32),
            jax.ShapeDtypeStruct((8, 64), F32),
        ),
        in_specs=[vmem] * 13,
        out_specs=(vmem,) * 4,
        scratch_shapes=[
            pltpu.VMEM((EXD, BASIS, LOCAL), BF16),
            pltpu.VMEM((EXD, 8, BASIS), F32),
            pltpu.VMEM((6, ROWS, 128), F32),
            pltpu.VMEM((6, ROWS, 128), F32),
            pltpu.VMEM((6, ROWS, 128), F32),
            pltpu.VMEM((6, ROWS, 128), F32),
            pltpu.VMEM((ROWS, 128), F32),
            pltpu.VMEM((EXD * LOCAL, NODES), BF16),
            pltpu.VMEM((EXD * LOCAL, NODES), BF16),
            pltpu.VMEM((8, TPAD), jnp.int32),
            pltpu.VMEM((8, TPAD), F32),
            pltpu.VMEM((12, GRP, 256), F32),
            pltpu.VMEM((BASIS, BASIS), F32),
            pltpu.VMEM((8, BASIS), F32),
            pltpu.VMEM((8, 8, BASIS), F32),
            pltpu.VMEM((4, 8, BASIS), F32),
            pltpu.VMEM((4, 8, BASIS), F32),
            pltpu.VMEM((8, BASIS), F32),
            pltpu.VMEM((8, BASIS), F32),
            pltpu.VMEM((16, 8, BASIS), F32),
            pltpu.VMEM((16, 8, BASIS), F32),
            pltpu.VMEM((16, 8, 128), F32),
            pltpu.VMEM((8, 8, 128), F32),
            dma((6,)),
            dma((6,)),
            dma((6,)),
            dma((6,)),
            dma,
            dma,
            dma((15,)),
            dma((8,)),
            dma((4,)),
            dma((16,)),
            dma((15,)),
            dma((4,)),
            dma((4,)),
            dma((16,)),
            dma((15,)),
            dma((4,)),
            dma((15,)),
            dma((16,)),
            dma((7,)),
            dma((8,)),
        ],
        compiler_params=pltpu.CompilerParams(collective_id=0, has_side_effects=True),
        name="backward_window",
    )(
        state.reshape(EXD * LOCAL, FAC),
        basis_projection_weight,
        factor_node_loading,
        curve.reshape(1, NODES),
        discount,
        region.transpose(0, 2, 1),
        carry_in.T,
        group_of,
        swap_start,
        swap_length,
        strike,
        notional,
        bucket_map.T,
    )
    values, coefficients, node, bucketed = pl.pallas_call(
        finish,
        out_shape=(
            jax.ShapeDtypeStruct((GRP, LOCAL), F32),
            jax.ShapeDtypeStruct((EXD, GRP, BASIS), F32),
            jax.ShapeDtypeStruct((NODES,), F32),
            jax.ShapeDtypeStruct((64,), F32),
        ),
        in_specs=[vmem] * 4,
        out_specs=(vmem,) * 4,
        name="finish",
    )(values, coefficients, node, bucketed)
    return (values.T, coefficients, node, bucketed)


def solution(mesh):
    torus = Mesh(
        mesh.devices.reshape(2, 4, 2, 2, 4), ("path_0", "path_1", "path_2", "trade_0", "trade_1")
    )
    in_specs = (
        P(None, PATH, None),
        P(),
        P(),
        P(),
        P(None, PATH),
        P(None, PATH, TRADE),
        P(PATH, TRADE),
        P(TRADE),
        P(TRADE),
        P(TRADE),
        P(TRADE),
        P(TRADE),
        P(),
    )
    out_specs = (P(PATH, TRADE), P(None, TRADE, None), P(), P())
    return jax.shard_map(
        shards, mesh=torus, in_specs=in_specs, out_specs=out_specs, check_vma=False
    )
```

time: 1030 us -> 73.5 us (0.07)
  other arithmetic: 679 us -> 0 us
  matrix products: 95.5 us -> 0 us
  waiting for transfers between devices: 93 us -> 0 us
  Pallas kernels: 0 us -> 72.7 us
  blocking collectives: 64.8 us -> 0 us
  local copies, waits for them, and re-layouts: 43.1 us -> 0 us
  starting transfers between devices: 29.4 us -> 0 us
  between operations: 14.9 us -> 0.64 us
    another operation x43 -> x0, other arithmetic: 666 us -> none  [the longest x22 415 us: shards(): lower_factor = jnp.linalg.cholesky(grams + ridge_term[None])]
    psum x1 -> x0, waiting for transfers between devices: 83.7 us -> none  [shards(): lax.psum((stacked, local_projection(EXD - 1, final_target_value)), PATH)]
    pallas_call x0 -> x2, Pallas kernels: none -> 72.7 us  [the longest x1 71.3 us: shards(): pl.pallas_call(kernel, out_shape=(jax.ShapeDtypeStruct((GRP, LOCAL), F32)...]
    psum x6 -> x0, blocking collectives: 64.8 us -> none  [the longest x1 33.1 us: shards(): lax.psum((stacked, local_projection(EXD - 1, final_target_value)), PATH)]
    dot_general x25 -> x0, matrix products: 52.1 us -> none  [the longest x3 14.7 us: shards(): jnp.dot(node_df[moment_matrix], group_cash.T, precision=lax.Precision.HIG...]
    another operation x36 -> x0, matrix products: 43.4 us -> none  [the longest x15 16.1 us: solve_groups(): lax.linalg.triangular_solve(lower_factor, middle, left_side=True, lower=T...]
    all_to_all x4 -> x0, starting transfers between devices: 29.3 us -> none  [copy_for_each(): return lax.all_to_all(copies, axis, split_axis=0, concat_axis=0, tiled=True)]
    another operation x34 -> x0, local copies, waits for them, and re-layouts: 28.1 us -> none  [the longest x22 23.1 us: solve_groups(): lax.linalg.triangular_solve(lower_factor, middle, left_side=True, lower=T...]
  transfers between devices with their start and end apart: 5 -> 0, of which waited for: 3 -> 0; matrix products, arithmetic and copies ran while one was open for 6% -> 0% of each run, Pallas kernels for 0% -> 0%
where the time goes in v1:
time: 73.5 us; the launch traced here: 73.3 us
  Pallas kernels  72.7 us (99%)
    pallas_call x1, Pallas kernels, shards(): pl.pallas_call(kernel, out_shape=(jax.ShapeDtypeStruct((GRP, LOCAL), F32)...  71.3 us

profile of v1, /device:TPU:1, one launch (start us, length us, event | category | flops | bytes accessed | tf_op | source)
XLA Modules:
  0.0 73.3 jit_solution(11086331784931222649)
XLA Ops:
  0.6 71.3 %backward_window.1 = (f32[4,1024]{1,0:T(4,128)}, f32[3,4,256]{2,1,0:T(4,128)}, f32[8,128]{1,0:T(8,128)}, f32[8,64]{1,0:T(8,128)}) custom-call(bf16[3072,128]{1,0:T(8,128)(2,1)} %bitcast.6, bf16[128,256]{1,0:T(8,128)(2,1)} %weight.1, bf16[128,1024]{1,0:T(8,128)(2,1)} %loading.1, f32[1,1024]{1,0:T(1,128)} %bitcast.10, f32[3,1024]{1,0:T(4,128)} %discount.1, ...), custom_call_target="tpu_custom_call" | custom-call | tf_op jit(solution)/shard_map/backward_window/pallas_call | solution.py:578
  72.0 1.4 %finish.1 = (f32[4,1024]{1,0:T(4,128)}, f32[3,4,256]{2,1,0:T(4,128)}, f32[1024]{0:T(1024)}, f32[64]{0:T(128)}) custom-call(f32[4,1024]{1,0:T(4,128)} %get-tuple-element.12.values, f32[3,4,256]{2,1,0:T(4,128)} %get-tuple-element.13.coefficients, f32[8,128]{1,0:T(8,128)} %get-tuple-element.14.node, f32[8,64]{1,0:T(8,128)} %get-tuple-element.15.bucketed), custom_call_target="tpu_custom_call" | custom-call | tf_op jit(solution)/shard_map/finish/pallas_call | solution.py:650

commit v2 on v1

--- a/solution.py
+++ b/solution.py
@@ -22,6 +22,7 @@
 F32 = jnp.float32
 BF16 = jnp.bfloat16
 ROWS = 264
+DATES = (2, 0, 1)
 
 ridge_share = 0.05
 horizon = 30.0
@@ -104,8 +105,7 @@
     away,
     home,
     got_core,
-    got_z,
-    got_y,
+    got,
     df_hi,
     df_lo,
     ints,
@@ -124,10 +124,8 @@
     node_two,
     core_send,
     core_recv,
-    z_send,
-    z_recv,
-    y_send,
-    y_recv,
+    owner_send,
+    owner_recv,
     a_send,
     a_recv,
     b_send,
@@ -169,13 +167,12 @@
     for k in range(1, 8):
         pl.semaphore_signal(barrier, inc=1, device_id=trade_id((tme + k) % 8), device_id_type=MESH)
 
-    def features(i, _):
-        chunk = state[pl.ds(pl.multiple_of(i * 256, 256), 256), :]
-        wide = lax.dot_general(weight[...], chunk, (((0,), (1,)), ((), ())), preferred_element_type=F32)
-        ft[i // 4, :, pl.ds(pl.multiple_of((i % 4) * 256, 256), 256)] = jnp.tanh(wide).astype(BF16)
-        return 0
-
-    lax.fori_loop(0, 12, features, 0)
+    weight_t = weight[...].T
+
+    def features(d):
+        for c in range(4):
+            chunk = state[d * LOCAL + c * 256 : d * LOCAL + c * 256 + 256, :]
+            ft[d, :, c * 256 : c * 256 + 256] = jnp.tanh(dot(weight_t, chunk, NT)).astype(BF16)
 
     def masks(d):
         r = region[d]
@@ -190,64 +187,76 @@
         return dot(rows8.astype(BF16), ft[d], NT)
 
     zero4 = jnp.zeros((4, LOCAL), F32)
+    bar0 = jnp.full((4, LOCAL), 1.0 / PATHS, F32)
     target2 = discount[2:3, :] * carry[...]
-    rhs[2] = project(jnp.concatenate([masks(2)[0] * target2, zero4], axis=0), 2)
-    rhs[1] = jnp.zeros((8, BASIS), F32)
-    rhs[0] = project(jnp.concatenate([masks(0)[1] * (1.0 / PATHS), zero4], axis=0), 0)
+    in0, hold0, ex0, out0 = masks(0)
+    in1, hold1, ex1, out1 = masks(1)
+    in2, hold2, ex2, out2 = masks(2)
 
     r128 = lax.broadcasted_iota(jnp.int32, (128, 128), 0)
     c128 = lax.broadcasted_iota(jnp.int32, (128, 128), 1)
 
-    def gram(d, g, out, slot):
-        mask = jnp.where(region[d, pl.ds(g, 1), :] >= 1, 1.0, 0.0).astype(BF16)
-        f = ft[d]
-        masked = f * mask
-        top = dot(masked[0:128], f[0:128], NT)
-        low = dot(masked[128:256], f, NT)
+    def pack(out, slot, top, low, right):
         last = low[:, 128:256]
         out[slot, 0:128, :] = jnp.where(r128 >= c128, top, last)
         out[slot, 128:256, :] = low[:, 0:128]
         diagonal = jnp.sum(jnp.where(r128 == c128, last, 0.0), axis=0, keepdims=True)
-        right = rhs[d, pl.ds(g, 1), :]
         out[slot, 256:264, :] = jnp.concatenate(
             [diagonal, right[:, 0:128], right[:, 128:256], jnp.zeros((5, 128), F32)], axis=0
         )
 
-    pl.semaphore_wait(barrier, 22)
+    def grams(slot):
+        d = DATES[slot // 2]
+        j = yh if slot % 2 else 1 - yh
+        f = ft[d]
+        theirs = (1 - core) * 2 + j
+        ours = core * 2 + j
+        one = f * jnp.where(region[d, pl.ds(theirs, 1), :] >= 1, 1.0, 0.0).astype(BF16)
+        two = f * jnp.where(region[d, pl.ds(ours, 1), :] >= 1, 1.0, 0.0).astype(BF16)
+        top = dot(jnp.concatenate([one[0:128], two[0:128]], axis=0), f[0:128], NT)
+        low = dot(jnp.concatenate([one[128:256], two[128:256]], axis=0), f, NT)
+        pack(away, slot, top[0:128], low[0:128], rhs[d, pl.ds(theirs, 1), :])
+        pack(home, slot, top[128:256], low[128:256], rhs[d, pl.ds(ours, 1), :])
 
     def core_copy(i):
         return remote(away.at[i], got_core.at[i], core_send.at[i], core_recv.at[i], {"path_2": 1 - core})
 
-    def send_away(i, _):
-        gram(i // 2, (1 - core) * 2 + i % 2, away, i)
-        core_copy(i).start()
-        return 0
-
-    lax.fori_loop(0, 6, send_away, 0)
-
-    def keep_home(i, _):
-        gram(i // 2, core * 2 + i % 2, home, i)
-        return 0
-
-    lax.fori_loop(0, 6, keep_home, 0)
-
-    def z_copy(i, d):
-        slot = (z - d + 3) % 4
-        at = slot * 2 + i % 2
-        return remote(home.at[i], got_z.at[at], z_send.at[i], z_recv.at[at], {"path_1": d})
-
-    def send_z(i, _):
-        d = i // 2
+    def owner_copy(i):
+        d, other = DATES[i // 2], 1 - i % 2
+        at = 4 * other + (z - d + 4) % 4
+        to = {"path_0": 1 - yh if other else yh, "path_1": d}
+        return remote(home.at[i], got.at[at], owner_send.at[i], owner_recv.at[at], to)
+
+    def combine(i):
         core_copy(i).wait()
         home[i] = home[i] + got_core[i]
-
-        @pl.when(z != d)
-        def _():
-            z_copy(i, d).start()
-
-        return 0
-
-    lax.fori_loop(0, 6, send_z, 0)
+        if i % 2:
+
+            @pl.when(z != DATES[i // 2])
+            def _():
+                owner_copy(i).start()
+        else:
+            owner_copy(i).start()
+
+    rhs[1] = jnp.zeros((8, BASIS), F32)
+    features(2)
+    rhs[2] = project(jnp.concatenate([in2 * target2, zero4], axis=0), 2)
+    grams(0)
+    grams(1)
+    features(0)
+    rhs[0] = project(jnp.concatenate([hold0 * bar0, zero4], axis=0), 0)
+    grams(2)
+    grams(3)
+    pl.semaphore_wait(barrier, 22)
+    for i in range(4):
+        core_copy(i).start()
+    features(1)
+    grams(4)
+    core_copy(4).start()
+    for i in range(4):
+        combine(i)
+    grams(5)
+    core_copy(5).start()
 
     ints[...] = jnp.zeros_like(ints)
     floats[...] = jnp.zeros_like(floats)
@@ -290,18 +299,22 @@
     def sum3(t):
         return t[0:4] + t[4:8] + t[8:12]
 
-    def discounting(i, _):
-        span = pl.ds(pl.multiple_of(i * 256, 256), 256)
-        shock = dot(state[span, :], loading[...])
-        factor = jnp.exp(-times * (curve_row + shock))
-        hi = factor.astype(BF16)
-        lo = (factor - hi.astype(F32)).astype(BF16)
-        df_hi[span, :] = hi
-        df_lo[span, :] = lo
-        payoff[i] = sum3(dot(cash_stack, hi, NT) + dot(cash_stack, lo, NT))
-        return 0
-
-    lax.fori_loop(0, 12, discounting, 0)
+    def discounting(d):
+        def chunk(i, _):
+            span = pl.ds(pl.multiple_of(i * 256, 256), 256)
+            shock = dot(state[span, :], loading[...])
+            factor = jnp.exp(-times * (curve_row + shock))
+            hi = factor.astype(BF16)
+            lo = (factor - hi.astype(F32)).astype(BF16)
+            df_hi[span, :] = hi
+            df_lo[span, :] = lo
+            payoff[i] = sum3(dot(cash_stack, hi, NT) + dot(cash_stack, lo, NT))
+            return 0
+
+        lax.fori_loop(4 * d, 4 * d + 4, chunk, 0)
+
+    combine(4)
+    combine(5)
 
     def node_sum(w, d):
         stack = stack3(w)
@@ -309,45 +322,28 @@
         t = sum3(dot(stack, df_hi[span, :]) + dot(stack, df_lo[span, :]))
         return jnp.sum(cash * t, axis=0, keepdims=True)
 
-    @pl.when(z < 3)
-    def _():
-        for j in range(2):
-            total = home[z * 2 + j]
-            for slot in range(3):
-                z_copy_wait = remote(
-                    home.at[0], got_z.at[slot * 2 + j], z_send.at[0], z_recv.at[slot * 2 + j], {"path_1": 0}
-                )
-                z_copy_wait.wait_recv()
-                total = total + got_z[slot * 2 + j]
-            home[z * 2 + j] = total
-
-    def y_copy():
-        return remote(home.at[z * 2 + 1 - yh], got_y, y_send, y_recv, {"path_0": 1 - yh})
-
-    @pl.when(z < 3)
-    def _():
-        y_copy().start()
-
-    in0, hold0, ex0, out0 = masks(0)
-    bar0 = jnp.full((4, LOCAL), 1.0 / PATHS, F32)
-    node_total = node_sum(ex0 * bar0, 0)
-
-    def solve(rows8):
-        return dot(rows8, inverse_ref[...], NN, HIGH)
+    discounting(2)
+
+    discounting(0)
+
+    def solve(rows):
+        return dot(rows, inverse_ref[...], NN, HIGH)
+
+    def run(first, last, f):
+        def go(k, _):
+            f(k)
+            return 0
+
+        lax.fori_loop(first, last, go, 0)
+
+    def answer_copy(k, dst, sends, recvs, at):
+        return remote(answer_src, dst.at[at], sends.at[k - 1], recvs.at[at], path_id((me + k) % 16))
 
     def broadcast(dst, sends, recvs, at):
-        def go(k, _):
-            remote(answer_src, dst.at[at], sends.at[k - 1], recvs.at[at], path_id((me + k) % 16)).start()
-            return 0
-
-        lax.fori_loop(1, 16, go, 0)
+        run(1, 16, lambda k: answer_copy(k, dst, sends, recvs, at).start())
 
     def broadcast_done(dst, sends, recvs, at):
-        def go(k, _):
-            remote(answer_src, dst.at[at], sends.at[k - 1], recvs.at[at], path_id((me + k) % 16)).wait_send()
-            return 0
-
-        lax.fori_loop(1, 16, go, 0)
+        run(1, 16, lambda k: answer_copy(k, dst, sends, recvs, at).wait_send())
 
     def collect(dst, sends, recvs, at, owner):
         @pl.when(me != owner)
@@ -359,8 +355,10 @@
 
     @pl.when(z < 3)
     def _():
-        y_copy().wait()
-        packed = home[z * 2 + yh] + got_y[...]
+        packed = home[2 * ((z + 1) % 3) + 1]
+        for at in range(1, 8):
+            remote(home.at[0], got.at[at], owner_send.at[0], owner_recv.at[at], {"path_1": 0}).wait_recv()
+            packed = packed + got[at]
         mix = packed[0:128]
         flip = mix.T
         b = packed[128:256]
@@ -376,20 +374,20 @@
         def _():
             at = (1 - z // 2) * 4 + mine
             row = jnp.concatenate([packed[257:258], packed[258:259]], axis=1)
-            answer = solve(jnp.broadcast_to(row, (8, BASIS)))
+            answer = solve(jnp.broadcast_to(row, (2, BASIS)))
             answer_src[...] = answer
             answer_a[at] = answer
             broadcast(answer_a, a_send, a_recv, at)
 
+    node_total = node_sum(ex0 * bar0, 0)
+    discounting(1)
+
     for g in range(4):
         collect(answer_a, a_send, a_recv, g, owner_of(2, g))
         collect(answer_a, a_send, a_recv, 4 + g, owner_of(0, g))
 
     def pick(buffer, base, row):
-        return jnp.concatenate(
-            [buffer[base + g, row + (g if row >= 0 else 1) : row + (g if row >= 0 else 1) + 1, :] for g in range(4)],
-            axis=0,
-        )
+        return jnp.concatenate([buffer[base + g, row : row + 1, :] for g in range(4)], axis=0)
 
     def payoff_of(d):
         return jnp.concatenate([payoff[4 * d + k] for k in range(4)], axis=1)
@@ -398,46 +396,50 @@
         stacked = jnp.concatenate([coefficient, jnp.zeros_like(coefficient)], axis=0).astype(BF16)
         return dot(stacked, ft[d])[0:4]
 
-    coef2 = pick(answer_a, 0, -1)
-    back0 = pick(answer_a, 4, -1)
+    coef2 = pick(answer_a, 0, 0)
+    back0 = pick(answer_a, 4, 0)
     coefficient_out[2] = coef2
-    in1, hold1, ex1, out1 = masks(1)
-    in2, hold2, ex2, out2 = masks(2)
     values2 = ex2 * payoff_of(2) + hold2 * fit(coef2, 2) + out2 * target2
     bar1 = discount[0:1, :] * (out0 * bar0 + in0 * fit(back0, 0))
     target1 = discount[1:2, :] * values2
-    part_b[...] = project(jnp.concatenate([in1 * target1, hold1 * bar1], axis=0), 1)
-    gather_b[me] = part_b[...]
-
-    def gather(src, dst, sends, recvs, d):
+
+    def gather_copy(src, dst, sends, recvs, d, g):
+        return remote(src.at[g], dst.at[me], sends.at[g], recvs.at[me], path_id(owner_of(d, g)))
+
+    def gather(src, dst, sends, recvs, d, rows8):
         for g in range(4):
-            owner = owner_of(d, g)
-
-            @pl.when(me != owner)
+            src[g] = jnp.concatenate([rows8[g : g + 1], rows8[4 + g : 5 + g]], axis=0)
+        for g in range(4):
+
+            @pl.when(me != owner_of(d, g))
             def _():
-                remote(src, dst.at[me], sends.at[g], recvs.at[me], path_id(owner)).start()
+                gather_copy(src, dst, sends, recvs, d, g).start()
+
+        @pl.when(z == d)
+        def _():
+            dst[me] = src[mine]
 
     def gather_sent(src, dst, sends, recvs, d):
         for g in range(4):
-            owner = owner_of(d, g)
-
-            @pl.when(me != owner)
+
+            @pl.when(me != owner_of(d, g))
             def _():
-                remote(src, dst.at[me], sends.at[g], recvs.at[me], path_id(owner)).wait_send()
+                gather_copy(src, dst, sends, recvs, d, g).wait_send()
 
     def gathered(src, dst, sends, recvs):
-        def go(k, _):
+        def arrival(k):
             p = (me + k) % 16
-            remote(src, dst.at[p], sends.at[0], recvs.at[p], path_id(p)).wait_recv()
-            return 0
-
-        lax.fori_loop(1, 16, go, 0)
+            remote(src.at[0], dst.at[p], sends.at[0], recvs.at[p], path_id(p)).wait_recv()
+
+        run(1, 16, arrival)
         total = dst[0]
         for p in range(1, 16):
             total = total + dst[p]
         return total
 
-    gather(part_b, gather_b, b_send, b_recv, 1)
+    gather(
+        part_b, gather_b, b_send, b_recv, 1, project(jnp.concatenate([in1 * target1, hold1 * bar1], axis=0), 1)
+    )
     node_total = node_total + node_sum(ex1 * bar1, 1)
 
     @pl.when(z == 1)
@@ -450,13 +452,35 @@
     for g in range(4):
         collect(answer_b, bb_send, bb_recv, g, owner_of(1, g))
     coef1 = pick(answer_b, 0, 0)
-    back1 = pick(answer_b, 0, 4)
+    back1 = pick(answer_b, 0, 1)
     coefficient_out[1] = coef1
     values1 = ex1 * payoff_of(1) + hold1 * fit(coef1, 1) + out1 * target1
     target0 = discount[0:1, :] * values1
-    part_c[...] = project(jnp.concatenate([in0 * target0, zero4], axis=0), 0)
-    gather_c[me] = part_c[...]
-    gather(part_c, gather_c, c_send, c_recv, 0)
+    gather(part_c, gather_c, c_send, c_recv, 0, project(jnp.concatenate([in0 * target0, zero4], axis=0), 0))
+
+    bar2 = discount[1:2, :] * (out1 * bar1 + in1 * fit(back1, 1))
+    node_total = node_total + node_sum(ex2 * bar2, 2)
+    node_one[me] = jnp.concatenate([node_total[:, 128 * k : 128 * k + 128] for k in range(8)], axis=0)
+
+    def one_copy(k):
+        return remote(
+            node_one.at[me], node_one.at[me], n1_send.at[k - 1], n1_recv.at[me], path_id((me + k) % 16)
+        )
+
+    def one_arrival(k):
+        p = (me + k) % 16
+        return remote(node_one.at[me], node_one.at[p], n1_send.at[0], n1_recv.at[p], path_id(p))
+
+    def two_copy(k):
+        return remote(
+            node_two.at[tme], node_two.at[tme], n2_send.at[k - 1], n2_recv.at[tme], trade_id((tme + k) % 8)
+        )
+
+    def two_arrival(k):
+        t = (tme + k) % 8
+        return remote(node_two.at[tme], node_two.at[t], n2_send.at[0], n2_recv.at[t], trade_id(t))
+
+    run(1, 16, lambda k: one_copy(k).start())
 
     @pl.when(z == 0)
     def _():
@@ -466,37 +490,6 @@
         answer_c[mine] = answer
         broadcast(answer_c, cc_send, cc_recv, mine)
 
-    bar2 = discount[1:2, :] * (out1 * bar1 + in1 * fit(back1, 1))
-    node_total = node_total + node_sum(ex2 * bar2, 2)
-    tile = jnp.concatenate([node_total[:, 128 * k : 128 * k + 128] for k in range(8)], axis=0)
-    node_one[me] = tile
-
-    def one_copy(k):
-        return remote(
-            node_one.at[me], node_one.at[me], n1_send.at[k - 1], n1_recv.at[me], path_id((me + k) % 16)
-        )
-
-    def one_arrival(k):
-        p = (me + k) % 16
-        return remote(node_one.at[me], node_one.at[p], n1_send.at[0], n1_recv.at[p], path_id(p))
-
-    def two_copy(k):
-        return remote(
-            node_two.at[tme], node_two.at[tme], n2_send.at[k - 1], n2_recv.at[tme], trade_id((tme + k) % 8)
-        )
-
-    def two_arrival(k):
-        t = (tme + k) % 8
-        return remote(node_two.at[tme], node_two.at[t], n2_send.at[0], n2_recv.at[t], trade_id(t))
-
-    def run(first, last, f):
-        def go(k, _):
-            f(k)
-            return 0
-
-        lax.fori_loop(first, last, go, 0)
-
-    run(1, 16, lambda k: one_copy(k).start())
     run(1, 16, lambda k: one_arrival(k).wait_recv())
     total = node_one[0]
     for p in range(1, 16):
@@ -522,16 +515,14 @@
     line = jnp.concatenate([adjoint[k : k + 1, :] for k in range(8)], axis=1)
     bucket_out[...] = dot(jnp.broadcast_to(line, (8, NODES)), bucket_map[...], NT, HIGH)
 
-    def z_sent(i, _):
-        d = i // 2
-
-        @pl.when(z != d)
+    for i in (0, 2, 4):
+        owner_copy(i).wait_send()
+    for i in (1, 3, 5):
+
+        @pl.when(z != DATES[i // 2])
         def _():
-            z_copy(i, d).wait_send()
-
-        return 0
-
-    lax.fori_loop(0, 6, z_sent, 0)
+            owner_copy(i).wait_send()
+
     gather_sent(part_b, gather_b, b_send, b_recv, 1)
     gather_sent(part_c, gather_c, c_send, c_recv, 0)
 
@@ -591,30 +582,27 @@
             pltpu.VMEM((6, ROWS, 128), F32),
             pltpu.VMEM((6, ROWS, 128), F32),
             pltpu.VMEM((6, ROWS, 128), F32),
-            pltpu.VMEM((6, ROWS, 128), F32),
-            pltpu.VMEM((ROWS, 128), F32),
+            pltpu.VMEM((8, ROWS, 128), F32),
             pltpu.VMEM((EXD * LOCAL, NODES), BF16),
             pltpu.VMEM((EXD * LOCAL, NODES), BF16),
             pltpu.VMEM((8, TPAD), jnp.int32),
             pltpu.VMEM((8, TPAD), F32),
             pltpu.VMEM((12, GRP, 256), F32),
             pltpu.VMEM((BASIS, BASIS), F32),
-            pltpu.VMEM((8, BASIS), F32),
-            pltpu.VMEM((8, 8, BASIS), F32),
-            pltpu.VMEM((4, 8, BASIS), F32),
-            pltpu.VMEM((4, 8, BASIS), F32),
-            pltpu.VMEM((8, BASIS), F32),
-            pltpu.VMEM((8, BASIS), F32),
-            pltpu.VMEM((16, 8, BASIS), F32),
-            pltpu.VMEM((16, 8, BASIS), F32),
+            pltpu.VMEM((2, BASIS), F32),
+            pltpu.VMEM((8, 2, BASIS), F32),
+            pltpu.VMEM((4, 2, BASIS), F32),
+            pltpu.VMEM((4, 2, BASIS), F32),
+            pltpu.VMEM((4, 2, BASIS), F32),
+            pltpu.VMEM((4, 2, BASIS), F32),
+            pltpu.VMEM((16, 2, BASIS), F32),
+            pltpu.VMEM((16, 2, BASIS), F32),
             pltpu.VMEM((16, 8, 128), F32),
             pltpu.VMEM((8, 8, 128), F32),
             dma((6,)),
             dma((6,)),
             dma((6,)),
-            dma((6,)),
-            dma,
-            dma,
+            dma((8,)),
             dma((15,)),
             dma((8,)),
             dma((4,)),

time: 73.5 us -> 60.5 us (0.82)
  Pallas kernels: 72.7 us -> 59.7 us
    pallas_call x1, Pallas kernels: 71.3 us -> 58.3 us  [shards(): pl.pallas_call(kernel, out_shape=(jax.ShapeDtypeStruct((GRP, LOCAL), F32)...]
where the time goes in v2:
time: 60.5 us; the launch traced here: 60.3 us
  Pallas kernels  59.7 us (99%)
  between operations  0.64 us (1%)
    pallas_call x1, Pallas kernels, shards(): pl.pallas_call(kernel, out_shape=(jax.ShapeDtypeStruct((GRP, LOCAL), F32)...  58.3 us
    pallas_call x1, Pallas kernels, shards(): pl.pallas_call(finish, out_shape=(jax.ShapeDtypeStruct((GRP, LOCAL), F32)...  1.36 us

profile of v2, /device:TPU:1, one launch (start us, length us, event | category | flops | bytes accessed | tf_op | source)
XLA Modules:
  0.0 60.3 jit_solution(4823648793579908257)
XLA Ops:
  0.6 58.3 %backward_window.1 = (f32[4,1024]{1,0:T(4,128)}, f32[3,4,256]{2,1,0:T(4,128)}, f32[8,128]{1,0:T(8,128)}, f32[8,64]{1,0:T(8,128)}) custom-call(bf16[3072,128]{1,0:T(8,128)(2,1)} %bitcast.6, bf16[128,256]{1,0:T(8,128)(2,1)} %weight.1, bf16[128,1024]{1,0:T(8,128)(2,1)} %loading.1, f32[1,1024]{1,0:T(1,128)} %bitcast.10, f32[3,1024]{1,0:T(4,128)} %discount.1, ...), custom_call_target="tpu_custom_call" | custom-call | tf_op jit(solution)/shard_map/backward_window/pallas_call | solution.py:569
  59.0 1.4 %finish.1 = (f32[4,1024]{1,0:T(4,128)}, f32[3,4,256]{2,1,0:T(4,128)}, f32[1024]{0:T(1024)}, f32[64]{0:T(128)}) custom-call(f32[4,1024]{1,0:T(4,128)} %get-tuple-element.12.values, f32[3,4,256]{2,1,0:T(4,128)} %get-tuple-element.13.coefficients, f32[8,128]{1,0:T(8,128)} %get-tuple-element.14.node, f32[8,64]{1,0:T(8,128)} %get-tuple-element.15.bucketed), custom_call_target="tpu_custom_call" | custom-call | tf_op jit(solution)/shard_map/finish/pallas_call | solution.py:638

commit v3 on v2

--- a/solution.py
+++ b/solution.py
@@ -23,6 +23,11 @@
 BF16 = jnp.bfloat16
 ROWS = 264
 DATES = (2, 0, 1)
+FAR_FIRST = (12, 13, 11, 4, 5, 3, 10, 14, 9, 15, 8, 6, 2, 7, 1)
+
+
+def owner_z(d, j, core):
+    return {2: (j + core) % 2, 0: 2 + (j + core) % 2, 1: (1 - core) * (1 + j) + core * 3 * j}[d]
 
 ridge_share = 0.05
 horizon = 30.0
@@ -71,21 +76,23 @@
         lax.broadcasted_iota(jnp.int32, (BASIS, BASIS), 0) == lax.broadcasted_iota(jnp.int32, (BASIS, BASIS), 1)
     ).astype(F32)
     a = a * (1.0 / BOUND)
-    (alpha, beta), *others, last = polynomials()
+    (alpha, beta), *others, near, last = polynomials()
     inverse = alpha * eye - beta * a
     product = dot3(a, inverse)
     for alpha, beta in others:
         both = dot3(jnp.concatenate([inverse, product], axis=0), alpha * eye - beta * product)
         inverse, product = both[:BASIS], both[BASIS:]
+    alpha, beta = near
+    inverse = dot3(inverse, alpha * eye - beta * product)
     alpha, beta = last
-    product = dot(a, inverse, NN, HIGH)
-    return dot(inverse, alpha * eye - beta * product, NN, HIGH) * (1.0 / BOUND)
+    rest = dot(a, inverse, NN, HIGH) - eye
+    return ((alpha - beta) * inverse - beta * dot3(inverse, rest)) * (1.0 / BOUND)
 
 
 def kernel(
-    state,
+    state_hbm,
     weight,
-    loading,
+    loading_hbm,
     curve,
     discount,
     region,
@@ -95,7 +102,7 @@
     swap_length,
     strike,
     notional,
-    bucket_map,
+    bucket_hbm,
     values_out,
     coefficient_out,
     node_out,
@@ -106,6 +113,9 @@
     home,
     got_core,
     got,
+    state,
+    loading,
+    bucket_map,
     df_hi,
     df_lo,
     ints,
@@ -126,6 +136,7 @@
     core_recv,
     owner_send,
     owner_recv,
+    load_sem,
     a_send,
     a_recv,
     b_send,
@@ -149,6 +160,7 @@
     me = yh * 8 + z * 2 + core
     tme = yl * 4 + x
     mine = core * 2 + yh
+    owns = {d: z == owner_z(d, yh, core) for d in range(EXD)}
 
     def path_id(p):
         return {"path_0": p // 8, "path_1": (p // 2) % 4, "path_2": p % 2}
@@ -160,6 +172,19 @@
         return pltpu.make_async_remote_copy(
             src_ref=src, dst_ref=dst, send_sem=send, recv_sem=recv, device_id=device, device_id_type=MESH
         )
+
+    def load_state(d):
+        rows = pl.ds(d * LOCAL, LOCAL)
+        return pltpu.make_async_copy(state_hbm.at[rows], state.at[rows], load_sem.at[d])
+
+    def load_other(k):
+        pair = ((loading_hbm, loading), (bucket_hbm, bucket_map))[k]
+        return pltpu.make_async_copy(*pair, load_sem.at[3 + k])
+
+    for d in DATES:
+        load_state(d).start()
+    load_other(0).start()
+    load_other(1).start()
 
     barrier = pltpu.get_barrier_semaphore()
     for k in range(1, 16):
@@ -170,6 +195,7 @@
     weight_t = weight[...].T
 
     def features(d):
+        load_state(d).wait()
         for c in range(4):
             chunk = state[d * LOCAL + c * 256 : d * LOCAL + c * 256 + 256, :]
             ft[d, :, c * 256 : c * 256 + 256] = jnp.tanh(dot(weight_t, chunk, NT)).astype(BF16)
@@ -222,9 +248,11 @@
         return remote(away.at[i], got_core.at[i], core_send.at[i], core_recv.at[i], {"path_2": 1 - core})
 
     def owner_copy(i):
-        d, other = DATES[i // 2], 1 - i % 2
-        at = 4 * other + (z - d + 4) % 4
-        to = {"path_0": 1 - yh if other else yh, "path_1": d}
+        other = 1 - i % 2
+        j = 1 - yh if other else yh
+        goal = owner_z(DATES[i // 2], j, core)
+        at = 4 * other + (z - goal + 4) % 4
+        to = {"path_0": j, "path_1": goal}
         return remote(home.at[i], got.at[at], owner_send.at[i], owner_recv.at[at], to)
 
     def combine(i):
@@ -232,9 +260,10 @@
         home[i] = home[i] + got_core[i]
         if i % 2:
 
-            @pl.when(z != DATES[i // 2])
+            @pl.when(z != owner_z(DATES[i // 2], yh, core))
             def _():
                 owner_copy(i).start()
+
         else:
             owner_copy(i).start()
 
@@ -258,6 +287,9 @@
     grams(5)
     core_copy(5).start()
 
+    combine(4)
+    combine(5)
+
     ints[...] = jnp.zeros_like(ints)
     floats[...] = jnp.zeros_like(floats)
     starts, amounts = swap_start[...].reshape(1, TRADES), notional[...].reshape(1, TRADES)
@@ -299,7 +331,7 @@
     def sum3(t):
         return t[0:4] + t[4:8] + t[8:12]
 
-    def discounting(d):
+    def discounting(first, last):
         def chunk(i, _):
             span = pl.ds(pl.multiple_of(i * 256, 256), 256)
             shock = dot(state[span, :], loading[...])
@@ -311,10 +343,7 @@
             payoff[i] = sum3(dot(cash_stack, hi, NT) + dot(cash_stack, lo, NT))
             return 0
 
-        lax.fori_loop(4 * d, 4 * d + 4, chunk, 0)
-
-    combine(4)
-    combine(5)
+        lax.fori_loop(first, last, chunk, 0)
 
     def node_sum(w, d):
         stack = stack3(w)
@@ -322,9 +351,10 @@
         t = sum3(dot(stack, df_hi[span, :]) + dot(stack, df_lo[span, :]))
         return jnp.sum(cash * t, axis=0, keepdims=True)
 
-    discounting(2)
-
-    discounting(0)
+    load_other(0).wait()
+    discounting(8, 12)
+
+    discounting(0, 2)
 
     def solve(rows):
         return dot(rows, inverse_ref[...], NN, HIGH)
@@ -340,7 +370,8 @@
         return remote(answer_src, dst.at[at], sends.at[k - 1], recvs.at[at], path_id((me + k) % 16))
 
     def broadcast(dst, sends, recvs, at):
-        run(1, 16, lambda k: answer_copy(k, dst, sends, recvs, at).start())
+        for k in FAR_FIRST:
+            answer_copy(k, dst, sends, recvs, at).start()
 
     def broadcast_done(dst, sends, recvs, at):
         run(1, 16, lambda k: answer_copy(k, dst, sends, recvs, at).wait_send())
@@ -351,14 +382,21 @@
             remote(answer_src, dst.at[at], sends.at[0], recvs.at[at], path_id(owner)).wait_recv()
 
     def owner_of(d, g):
-        return (g % 2) * 8 + d * 2 + g // 2
-
-    @pl.when(z < 3)
+        return (g % 2) * 8 + owner_z(d, g % 2, g // 2) * 2 + g // 2
+
+    for place, d in enumerate(DATES):
+
+        @pl.when(owns[d])
+        def _():
+            packed = home[2 * place + 1]
+            for at in range(1, 8):
+                remote(home.at[0], got.at[at], owner_send.at[0], owner_recv.at[at], {"path_1": 0}).wait_recv()
+                packed = packed + got[at]
+            got[0] = packed
+
+    @pl.when(owns[0] | owns[1] | owns[2])
     def _():
-        packed = home[2 * ((z + 1) % 3) + 1]
-        for at in range(1, 8):
-            remote(home.at[0], got.at[at], owner_send.at[0], owner_recv.at[at], {"path_1": 0}).wait_recv()
-            packed = packed + got[at]
+        packed = got[0]
         mix = packed[0:128]
         flip = mix.T
         b = packed[128:256]
@@ -370,17 +408,17 @@
         )
         inverse_ref[...] = invert(full)
 
-        @pl.when(z != 1)
+        row = jnp.concatenate([packed[257:258], packed[258:259]], axis=1)
+        answer_src[...] = solve(jnp.broadcast_to(row, (2, BASIS)))
+
+    for base, d in ((0, 2), (4, 0)):
+
+        @pl.when(owns[d])
         def _():
-            at = (1 - z // 2) * 4 + mine
-            row = jnp.concatenate([packed[257:258], packed[258:259]], axis=1)
-            answer = solve(jnp.broadcast_to(row, (2, BASIS)))
-            answer_src[...] = answer
-            answer_a[at] = answer
-            broadcast(answer_a, a_send, a_recv, at)
-
-    node_total = node_sum(ex0 * bar0, 0)
-    discounting(1)
+            broadcast(answer_a, a_send, a_recv, base + mine)
+            answer_a[base + mine] = answer_src[...]
+
+    discounting(4, 8)
 
     for g in range(4):
         collect(answer_a, a_send, a_recv, g, owner_of(2, g))
@@ -415,7 +453,7 @@
             def _():
                 gather_copy(src, dst, sends, recvs, d, g).start()
 
-        @pl.when(z == d)
+        @pl.when(owns[d])
         def _():
             dst[me] = src[mine]
 
@@ -440,9 +478,10 @@
     gather(
         part_b, gather_b, b_send, b_recv, 1, project(jnp.concatenate([in1 * target1, hold1 * bar1], axis=0), 1)
     )
-    node_total = node_total + node_sum(ex1 * bar1, 1)
-
-    @pl.when(z == 1)
+    discounting(2, 4)
+    node_total = node_sum(ex0 * bar0, 0) + node_sum(ex1 * bar1, 1)
+
+    @pl.when(owns[1])
     def _():
         answer = solve(gathered(part_b, gather_b, b_send, b_recv))
         answer_src[...] = answer
@@ -482,7 +521,7 @@
 
     run(1, 16, lambda k: one_copy(k).start())
 
-    @pl.when(z == 0)
+    @pl.when(owns[0])
     def _():
         answer = solve(gathered(part_c, gather_c, c_send, c_recv))
         broadcast_done(answer_a, a_send, a_recv, 4 + mine)
@@ -512,6 +551,7 @@
     ).astype(F32)
     adjoint = -((grid + 1.0) * (horizon / NODES)) * total
     node_out[...] = adjoint
+    load_other(1).wait()
     line = jnp.concatenate([adjoint[k : k + 1, :] for k in range(8)], axis=1)
     bucket_out[...] = dot(jnp.broadcast_to(line, (8, NODES)), bucket_map[...], NT, HIGH)
 
@@ -519,22 +559,22 @@
         owner_copy(i).wait_send()
     for i in (1, 3, 5):
 
-        @pl.when(z != DATES[i // 2])
+        @pl.when(z != owner_z(DATES[i // 2], yh, core))
         def _():
             owner_copy(i).wait_send()
 
     gather_sent(part_b, gather_b, b_send, b_recv, 1)
     gather_sent(part_c, gather_c, c_send, c_recv, 0)
 
-    @pl.when(z == 2)
+    @pl.when(owns[2])
     def _():
         broadcast_done(answer_a, a_send, a_recv, mine)
 
-    @pl.when(z == 1)
+    @pl.when(owns[1])
     def _():
         broadcast_done(answer_b, bb_send, bb_recv, mine)
 
-    @pl.when(z == 0)
+    @pl.when(owns[0])
     def _():
         broadcast_done(answer_c, cc_send, cc_recv, mine)
 
@@ -565,6 +605,7 @@
     bucket_map,
 ):
     vmem = pl.BlockSpec(memory_space=pltpu.VMEM)
+    anywhere = pl.BlockSpec(memory_space=pl.ANY)
     dma = pltpu.SemaphoreType.DMA
     values, coefficients, node, bucketed = pl.pallas_call(
         kernel,
@@ -574,7 +615,7 @@
             jax.ShapeDtypeStruct((8, 128), F32),
             jax.ShapeDtypeStruct((8, 64), F32),
         ),
-        in_specs=[vmem] * 13,
+        in_specs=[anywhere, vmem, anywhere, *[vmem] * 9, anywhere],
         out_specs=(vmem,) * 4,
         scratch_shapes=[
             pltpu.VMEM((EXD, BASIS, LOCAL), BF16),
@@ -583,6 +624,9 @@
             pltpu.VMEM((6, ROWS, 128), F32),
             pltpu.VMEM((6, ROWS, 128), F32),
             pltpu.VMEM((8, ROWS, 128), F32),
+            pltpu.VMEM((EXD * LOCAL, FAC), BF16),
+            pltpu.VMEM((FAC, NODES), BF16),
+            pltpu.VMEM((64, NODES), F32),
             pltpu.VMEM((EXD * LOCAL, NODES), BF16),
             pltpu.VMEM((EXD * LOCAL, NODES), BF16),
             pltpu.VMEM((8, TPAD), jnp.int32),
@@ -603,6 +647,7 @@
             dma((6,)),
             dma((6,)),
             dma((8,)),
+            dma((5,)),
             dma((15,)),
             dma((8,)),
             dma((4,)),

time: 60.5 us -> 58.1 us (0.960)
  Pallas kernels: 59.7 us -> 57.2 us
    pallas_call x1, Pallas kernels: 58.3 us -> 55.9 us  [shards(): pl.pallas_call(kernel, out_shape=(jax.ShapeDtypeStruct((GRP, LOCAL), F32)...]
where the time goes in v3:
time: 58.1 us; the launch traced here: 57.9 us
  Pallas kernels  57.2 us (98%)
  between operations  0.64 us (1%)
    pallas_call x1, Pallas kernels, shards(): pl.pallas_call(kernel, out_shape=(jax.ShapeDtypeStruct((GRP, LOCAL), F32)...  55.9 us
    pallas_call x1, Pallas kernels, shards(): pl.pallas_call(finish, out_shape=(jax.ShapeDtypeStruct((GRP, LOCAL), F32)...  1.36 us

profile of v3, /device:TPU:1, one launch (start us, length us, event | category | flops | bytes accessed | tf_op | source)
XLA Modules:
  0.0 57.9 jit_solution(295555138601895245)
XLA Ops:
  0.6 55.9 %backward_window.1 = (f32[4,1024]{1,0:T(4,128)}, f32[3,4,256]{2,1,0:T(4,128)}, f32[8,128]{1,0:T(8,128)}, f32[8,64]{1,0:T(8,128)}) custom-call(bf16[3072,128]{1,0:T(8,128)(2,1)} %bitcast.6, bf16[128,256]{1,0:T(8,128)(2,1)} %weight.1, bf16[128,1024]{1,0:T(8,128)(2,1)} %loading_hbm.1, f32[1,1024]{1,0:T(1,128)} %bitcast.10, f32[3,1024]{1,0:T(4,128)} %discount.1, ...), custom_call_target="tpu_custom_call" | custom-call | tf_op jit(solution)/shard_map/backward_window/pallas_call | solution.py:610
  56.5 1.4 %finish.1 = (f32[4,1024]{1,0:T(4,128)}, f32[3,4,256]{2,1,0:T(4,128)}, f32[1024]{0:T(1024)}, f32[64]{0:T(128)}) custom-call(f32[4,1024]{1,0:T(4,128)} %get-tuple-element.12.values, f32[3,4,256]{2,1,0:T(4,128)} %get-tuple-element.13.coefficients, f32[8,128]{1,0:T(8,128)} %get-tuple-element.14.node, f32[8,64]{1,0:T(8,128)} %get-tuple-element.15.bucketed), custom_call_target="tpu_custom_call" | custom-call | tf_op jit(solution)/shard_map/finish/pallas_call | solution.py:683

commit v4 on v3

--- a/solution.py
+++ b/solution.py
@@ -287,9 +287,6 @@
     grams(5)
     core_copy(5).start()
 
-    combine(4)
-    combine(5)
-
     ints[...] = jnp.zeros_like(ints)
     floats[...] = jnp.zeros_like(floats)
     starts, amounts = swap_start[...].reshape(1, TRADES), notional[...].reshape(1, TRADES)
@@ -355,6 +352,8 @@
     discounting(8, 12)
 
     discounting(0, 2)
+    combine(4)
+    combine(5)
 
     def solve(rows):
         return dot(rows, inverse_ref[...], NN, HIGH)
@@ -384,18 +383,14 @@
     def owner_of(d, g):
         return (g % 2) * 8 + owner_z(d, g % 2, g // 2) * 2 + g // 2
 
-    for place, d in enumerate(DATES):
-
-        @pl.when(owns[d])
-        def _():
-            packed = home[2 * place + 1]
-            for at in range(1, 8):
-                remote(home.at[0], got.at[at], owner_send.at[0], owner_recv.at[at], {"path_1": 0}).wait_recv()
-                packed = packed + got[at]
-            got[0] = packed
-
-    @pl.when(owns[0] | owns[1] | owns[2])
-    def _():
+    def arrive(place):
+        packed = home[2 * place + 1]
+        for at in range(1, 8):
+            remote(home.at[0], got.at[at], owner_send.at[0], owner_recv.at[at], {"path_1": 0}).wait_recv()
+            packed = packed + got[at]
+        got[0] = packed
+
+    def invert_sum():
         packed = got[0]
         mix = packed[0:128]
         flip = mix.T
@@ -408,7 +403,16 @@
         )
         inverse_ref[...] = invert(full)
 
-        row = jnp.concatenate([packed[257:258], packed[258:259]], axis=1)
+    for place in range(2):
+
+        @pl.when(owns[DATES[place]])
+        def _():
+            arrive(place)
+
+    @pl.when(owns[0] | owns[2])
+    def _():
+        invert_sum()
+        row = jnp.concatenate([got[0, 257:258], got[0, 258:259]], axis=1)
         answer_src[...] = solve(jnp.broadcast_to(row, (2, BASIS)))
 
     for base, d in ((0, 2), (4, 0)):
@@ -419,6 +423,11 @@
             answer_a[base + mine] = answer_src[...]
 
     discounting(4, 8)
+
+    @pl.when(owns[1])
+    def _():
+        arrive(2)
+        invert_sum()
 
     for g in range(4):
         collect(answer_a, a_send, a_recv, g, owner_of(2, g))

time: 58.1 us -> 54.6 us (0.940)
  Pallas kernels: 57.2 us -> 53.7 us
    pallas_call x1, Pallas kernels: 55.9 us -> 52.3 us  [shards(): pl.pallas_call(kernel, out_shape=(jax.ShapeDtypeStruct((GRP, LOCAL), F32)...]
where the time goes in v4:
time: 54.6 us; the launch traced here: 54.4 us
  Pallas kernels  53.7 us (98%)
  between operations  0.64 us (1%)
    pallas_call x1, Pallas kernels, shards(): pl.pallas_call(kernel, out_shape=(jax.ShapeDtypeStruct((GRP, LOCAL), F32)...  52.3 us
    pallas_call x1, Pallas kernels, shards(): pl.pallas_call(finish, out_shape=(jax.ShapeDtypeStruct((GRP, LOCAL), F32)...  1.36 us

profile of v4, /device:TPU:1, one launch (start us, length us, event | category | flops | bytes accessed | tf_op | source)
XLA Modules:
  0.0 54.4 jit_solution(966766062839562729)
XLA Ops:
  0.6 52.3 %backward_window.1 = (f32[4,1024]{1,0:T(4,128)}, f32[3,4,256]{2,1,0:T(4,128)}, f32[8,128]{1,0:T(8,128)}, f32[8,64]{1,0:T(8,128)}) custom-call(bf16[3072,128]{1,0:T(8,128)(2,1)} %bitcast.6, bf16[128,256]{1,0:T(8,128)(2,1)} %weight.1, bf16[128,1024]{1,0:T(8,128)(2,1)} %loading_hbm.1, f32[1,1024]{1,0:T(1,128)} %bitcast.10, f32[3,1024]{1,0:T(4,128)} %discount.1, ...), custom_call_target="tpu_custom_call" | custom-call | tf_op jit(solution)/shard_map/backward_window/pallas_call | solution.py:619
  53.0 1.4 %finish.1 = (f32[4,1024]{1,0:T(4,128)}, f32[3,4,256]{2,1,0:T(4,128)}, f32[1024]{0:T(1024)}, f32[64]{0:T(128)}) custom-call(f32[4,1024]{1,0:T(4,128)} %get-tuple-element.12.values, f32[3,4,256]{2,1,0:T(4,128)} %get-tuple-element.13.coefficients, f32[8,128]{1,0:T(8,128)} %get-tuple-element.14.node, f32[8,64]{1,0:T(8,128)} %get-tuple-element.15.bucketed), custom_call_target="tpu_custom_call" | custom-call | tf_op jit(solution)/shard_map/finish/pallas_call | solution.py:692
